TPU v7x, 32 devices: a whole 2x2x4 slice. The times are simulated.
32 devices in a mesh: fsdp: 8 (over z, x), ctx: 4 (over y, core).
Axes of the slice: x: 2, y: 2, z: 4, core: 2. Of those that a mesh axis runs over, the one named last changes fastest.
Arguments:
- inputs: bfloat16 [8, 1024, 2048], P('fsdp', 'ctx'), may hold values from -6 to 6
- cotangent: bfloat16 [8, 1024, 2048], P('fsdp', 'ctx'), may hold values from -6 to 6
- lengths: int32 [8], P('fsdp'), may hold values from 1024 to 1024, as said below
- qkv_weight: bfloat16 [2048, 1536], P('fsdp'), may hold values from -0.125 to 0.125
- out_weight: bfloat16 [1024, 2048], P('fsdp'), may hold values from -3 to 3
- gate_up: bfloat16 [2048, 2, 4096], P('fsdp'), may hold values from -0.125 to 0.125
- down_weight: bfloat16 [4096, 2048], P('fsdp'), may hold values from -0.09375 to 0.09375
- attn_gain: bfloat16 [2048], P('fsdp'), may hold values from 0.5 to 1.5
- ffn_gain: bfloat16 [2048], P('fsdp'), may hold values from 0.5 to 1.5
- qk_gain: bfloat16 [2, 64], replicated, may hold values from 0.5 to 1.5
Outputs:
- layer_out: bfloat16 [8, 1024, 2048], P('fsdp', 'ctx')
- input_grad: bfloat16 [8, 1024, 2048], P('fsdp', 'ctx')
- qkv_grad: float32 [2048, 1536], P('fsdp')
- out_grad: float32 [1024, 2048], P('fsdp')
- gate_up_grad: float32 [2048, 2, 4096], P('fsdp')
- down_grad: float32 [4096, 2048], P('fsdp')
- attn_gain_grad: float32 [2048], P('fsdp')
- ffn_gain_grad: float32 [2048], P('fsdp')
- qk_gain_grad: float32 [2, 64], replicated
Inputs may be any that keep to these rules, and one draw needn't show every extreme that they name: `lengths`: valid length of each slot; some slot is full, of length 1024.
All inputs are finite; a program needn't handle non-finite values.
Results may differ from a plain program's by a relative error of at most 0.02.
Values may be sent and summed in bfloat16 or wider, within the bound.
A program may use at most 384 MiB of HBM per device.

v0:
```python
import math
import jax
import jax.numpy as jnp
from jax import lax
from jax.sharding import PartitionSpec as P

HEADS = 16
KV_HEADS = 4
HEAD_DIM = 64
EPSILON = 1e-06


def root_norm(values, norm_gain):
    factor = lax.rsqrt(jnp.mean(values * values, axis=-1, keepdims=True) + EPSILON)
    return values * factor * norm_gain


def rotation_tables(positions):
    half_dim = HEAD_DIM // 2
    frequency = 10000.0 ** (-(2.0 * jnp.arange(half_dim, dtype=jnp.float32)) / HEAD_DIM)
    angles = positions.astype(jnp.float32)[:, None] * frequency[None, :]
    return (jnp.cos(angles), jnp.sin(angles))


def rotate(values, cos_table, sin_table):
    half_dim = values.shape[-1] // 2
    lower_half = values[..., :half_dim]
    upper_half = values[..., half_dim:]
    cos_part = cos_table[:, None, :]
    sin_part = sin_table[:, None, :]
    return jnp.concatenate(
        [
            lower_half * cos_part - upper_half * sin_part,
            upper_half * cos_part + lower_half * sin_part,
        ],
        axis=-1,
    )


def prepare_heads(qkv_out, head_gain, cos_table, sin_table):
    row_count = qkv_out.shape[0]
    query_cols = HEADS * HEAD_DIM
    key_cols = KV_HEADS * HEAD_DIM
    queries = qkv_out[:, :query_cols].reshape(row_count, HEADS, HEAD_DIM)
    key_part = qkv_out[:, query_cols : query_cols + key_cols].reshape(row_count, KV_HEADS, HEAD_DIM)
    value_part = qkv_out[:, query_cols + key_cols :]
    queries = rotate(root_norm(queries, head_gain[0]), cos_table, sin_table).reshape(
        row_count, query_cols
    )
    key_part = rotate(root_norm(key_part, head_gain[1]), cos_table, sin_table).reshape(
        row_count, key_cols
    )
    return (queries, key_part, value_part)


def activate(projected):
    gate_part = projected[:, 0]
    return gate_part * jax.nn.sigmoid(gate_part) * projected[:, 1]


def contract_rows(left, right):
    return lax.dot_general(
        left, right, (((0,), (0,)), ((), ())), preferred_element_type=jnp.float32
    )


def contract_cols(left, right):
    return lax.dot_general(
        left, right, (((1,), (1,)), ((), ())), preferred_element_type=jnp.float32
    )


def on_device(
    inputs,
    cotangent,
    lengths,
    qkv_weight,
    out_weight,
    gate_up,
    down_weight,
    attn_gain,
    ffn_gain,
    qk_gain,
):
    token_count = inputs.shape[1]
    group = HEADS // KV_HEADS
    key_cols = KV_HEADS * HEAD_DIM
    seq_len = token_count * lax.axis_size("ctx")
    positions = lax.axis_index("ctx") * token_count + jnp.arange(token_count, dtype=jnp.int32)
    length = lengths[0]
    row_keep = (positions < length).astype(jnp.float32)[:, None]
    inv_root = 1.0 / math.sqrt(HEAD_DIM)
    source = inputs[0].astype(jnp.float32)
    qkv_full, out_full, attn_full, ffn_full = (
        lax.all_gather(qkv_weight, "fsdp", axis=0, tiled=True),
        lax.all_gather(out_weight, "fsdp", axis=0, tiled=True),
        lax.all_gather(attn_gain, "fsdp", axis=0, tiled=True),
        lax.all_gather(ffn_gain, "fsdp", axis=0, tiled=True),
    )
    attn_norm = attn_full.astype(jnp.float32)
    ffn_norm = ffn_full.astype(jnp.float32)
    normed = root_norm(source, attn_norm).astype(jnp.bfloat16)
    qkv_out = jnp.dot(normed, qkv_full, preferred_element_type=jnp.float32)
    cos_table, sin_table = rotation_tables(positions)
    head_gain = qk_gain.astype(jnp.float32)

    def head_pieces(qkv_values, gain_values):
        return prepare_heads(qkv_values, gain_values, cos_table, sin_table)

    head_values, head_pull = jax.vjp(head_pieces, qkv_out, head_gain)
    queries, key_part, value_part = head_values
    query_low = queries.astype(jnp.bfloat16).reshape(token_count, KV_HEADS, group, HEAD_DIM)
    kv_local = jnp.concatenate([key_part, value_part], axis=1).astype(jnp.bfloat16)
    kv_whole = lax.all_gather(kv_local, "ctx", axis=0, tiled=True)
    block = 512
    block_total = seq_len // block
    kv_blocks = kv_whole.reshape(block_total, block, 2, KV_HEADS, HEAD_DIM)
    starts = jnp.arange(block_total, dtype=jnp.int32) * block

    def block_scores(key_block, block_start):
        scores = (
            jnp.einsum("bhgd,thd->hgbt", query_low, key_block, preferred_element_type=jnp.float32)
            * inv_root
        )
        key_pos = block_start + jnp.arange(key_block.shape[0], dtype=jnp.int32)
        visible = (key_pos[None, :] <= positions[:, None]) & (key_pos[None, :] < length)
        return (scores, visible)

    def max_step(state, item):
        running_max, running_sum = state
        kv_block, block_start = item
        scores, visible = block_scores(kv_block[:, 0], block_start)
        new_max = jnp.maximum(running_max, jnp.max(jnp.where(visible, scores, -1e30), axis=-1))
        expanded = jnp.where(visible, jnp.exp(scores - new_max[..., None]), 0.0)
        running_sum = running_sum * jnp.exp(running_max - new_max) + jnp.sum(expanded, axis=-1)
        return ((new_max, running_sum), None)

    stat_shape = (KV_HEADS, group, token_count)
    start_state = (jnp.full(stat_shape, -1e30, jnp.float32), jnp.zeros(stat_shape, jnp.float32))
    final_state, unused_out = lax.scan(max_step, start_state, (kv_blocks, starts))
    log_total = final_state[0] + jnp.log(final_state[1])

    def block_probs(kv_block, block_start):
        scores, visible = block_scores(kv_block[:, 0], block_start)
        return jnp.where(visible, jnp.exp(scores - log_total[..., None]), 0.0)

    def value_step(totals, item):
        kv_block, block_start = item
        probs_low = block_probs(kv_block, block_start).astype(jnp.bfloat16)
        return (
            totals
            + jnp.einsum(
                "hgbt,thd->bhgd", probs_low, kv_block[:, 1], preferred_element_type=jnp.float32
            ),
            None,
        )

    attended, unused_out = lax.scan(
        value_step,
        jnp.zeros((token_count, KV_HEADS, group, HEAD_DIM), jnp.float32),
        (kv_blocks, starts),
    )
    attended_low = attended.reshape(token_count, HEADS * HEAD_DIM).astype(jnp.bfloat16)
    middle = source + jnp.dot(attended_low, out_full, preferred_element_type=jnp.float32)
    normed_mid = root_norm(middle, ffn_norm).astype(jnp.bfloat16)
    columns = normed_mid
    projected = jnp.einsum(
        "td,dgf->tgf",
        columns,
        lax.all_gather(gate_up, "fsdp", axis=0, tiled=True),
        preferred_element_type=jnp.float32,
    )
    act_value, act_pull = jax.vjp(activate, projected)
    hidden = act_value.astype(jnp.bfloat16)
    columns = hidden
    ffn_out = jnp.dot(
        columns,
        lax.all_gather(down_weight, "fsdp", axis=0, tiled=True),
        preferred_element_type=jnp.float32,
    )
    layer_out = (row_keep * (middle + ffn_out)).astype(jnp.bfloat16)[None]
    d_out = row_keep * cotangent[0].astype(jnp.float32)
    d_out_low = d_out.astype(jnp.bfloat16)
    down_shard = lax.psum_scatter(
        contract_rows(hidden, d_out_low).astype(jnp.bfloat16),
        "fsdp",
        scatter_dimension=0,
        tiled=True,
    )
    d_hidden = contract_cols(d_out_low, lax.all_gather(down_weight, "fsdp", axis=0, tiled=True))
    d_proj_low = act_pull(d_hidden)[0].astype(jnp.bfloat16)
    columns = normed_mid
    gate_up_shard = lax.psum_scatter(
        jnp.einsum("td,tgf->dgf", columns, d_proj_low, preferred_element_type=jnp.float32).astype(
            jnp.bfloat16
        ),
        "fsdp",
        scatter_dimension=0,
        tiled=True,
    )
    d_normed_mid = jnp.einsum(
        "tgf,dgf->td",
        d_proj_low,
        lax.all_gather(gate_up, "fsdp", axis=0, tiled=True),
        preferred_element_type=jnp.float32,
    )
    mid_value, mid_pull = jax.vjp(root_norm, middle, ffn_norm)
    d_mid_norm, ffn_gain_part = mid_pull(d_normed_mid)
    d_middle = d_out + d_mid_norm
    d_branch = d_middle.astype(jnp.bfloat16)
    out_term = contract_rows(attended_low, d_branch)
    d_attended = (
        contract_cols(d_branch, out_full)
        .astype(jnp.bfloat16)
        .reshape(token_count, KV_HEADS, group, HEAD_DIM)
    )
    delta = jnp.transpose(jnp.sum(d_attended.astype(jnp.float32) * attended, axis=-1), (1, 2, 0))

    def block_grads(kv_block, block_start):
        probs = block_probs(kv_block, block_start)
        d_probs = jnp.einsum(
            "bhgd,thd->hgbt", d_attended, kv_block[:, 1], preferred_element_type=jnp.float32
        )
        d_scores = (probs * (d_probs - delta[..., None])).astype(jnp.bfloat16)
        return (probs.astype(jnp.bfloat16), d_scores)

    def query_step(totals, item):
        kv_block, block_start = item
        probs_low, d_scores = block_grads(kv_block, block_start)
        return (
            totals
            + jnp.einsum(
                "hgbt,thd->bhgd", d_scores, kv_block[:, 0], preferred_element_type=jnp.float32
            ),
            None,
        )

    d_query_sum, unused_out = lax.scan(
        query_step,
        jnp.zeros((token_count, KV_HEADS, group, HEAD_DIM), jnp.float32),
        (kv_blocks, starts),
    )
    d_query = (d_query_sum * inv_root).reshape(token_count, HEADS * HEAD_DIM).astype(jnp.bfloat16)
    sub_block = 512
    sub_total = token_count * lax.axis_size("ctx") // sub_block
    pieces = kv_whole.reshape(sub_total, sub_block, 2, KV_HEADS, HEAD_DIM)
    sub_starts = jnp.arange(sub_total, dtype=jnp.int32) * sub_block

    def key_grads(item):
        kv_block, block_start = item
        probs_low, d_scores = block_grads(kv_block, block_start)
        d_keys = (
            jnp.einsum("hgbt,bhgd->thd", d_scores, query_low, preferred_element_type=jnp.float32)
            * inv_root
        )
        d_values = jnp.einsum(
            "hgbt,bhgd->thd", probs_low, d_attended, preferred_element_type=jnp.float32
        )
        return jnp.concatenate(
            [d_keys.reshape(sub_block, key_cols), d_values.reshape(sub_block, key_cols)], axis=1
        )

    kv_grad = lax.psum_scatter(
        lax.map(key_grads, (pieces, sub_starts))
        .reshape(token_count * lax.axis_size("ctx"), 2 * key_cols)
        .astype(jnp.bfloat16),
        "ctx",
        scatter_dimension=0,
        tiled=True,
    ).astype(jnp.float32)
    d_key_low = kv_grad[:, :key_cols].astype(jnp.bfloat16).astype(jnp.float32)
    d_value_low = kv_grad[:, key_cols:].astype(jnp.bfloat16).astype(jnp.float32)
    d_qkv_out, qk_part = head_pull((d_query.astype(jnp.float32), d_key_low, d_value_low))
    d_qkv = d_qkv_out.astype(jnp.bfloat16)
    qkv_term = contract_rows(normed, d_qkv)
    d_normed = contract_cols(d_qkv, qkv_full)
    first_value, first_pull = jax.vjp(root_norm, source, attn_norm)
    d_source_norm, attn_gain_part = first_pull(d_normed)
    input_grad = (d_middle + d_source_norm).astype(jnp.bfloat16)[None]
    qkv_shard, out_shard, attn_shard, ffn_shard = (
        lax.psum_scatter(
            qkv_term.astype(jnp.bfloat16), "fsdp", scatter_dimension=0, tiled=True
        ).astype(jnp.float32),
        lax.psum_scatter(
            out_term.astype(jnp.bfloat16), "fsdp", scatter_dimension=0, tiled=True
        ).astype(jnp.float32),
        lax.psum_scatter(
            attn_gain_part.astype(jnp.bfloat16), "fsdp", scatter_dimension=0, tiled=True
        ).astype(jnp.float32),
        lax.psum_scatter(
            ffn_gain_part.astype(jnp.bfloat16), "fsdp", scatter_dimension=0, tiled=True
        ).astype(jnp.float32),
    )
    summed = (
        lax.psum(qkv_shard.astype(jnp.bfloat16), "ctx").astype(jnp.float32),
        lax.psum(out_shard.astype(jnp.bfloat16), "ctx").astype(jnp.float32),
        lax.psum(gate_up_shard, "ctx").astype(jnp.float32),
        lax.psum(down_shard, "ctx").astype(jnp.float32),
        lax.psum(attn_shard.astype(jnp.bfloat16), "ctx").astype(jnp.float32),
        lax.psum(ffn_shard.astype(jnp.bfloat16), "ctx").astype(jnp.float32),
    )
    qk_total = lax.psum(qk_part, ("fsdp", "ctx"))
    return (
        layer_out,
        input_grad,
        summed[0],
        summed[1],
        summed[2],
        summed[3],
        summed[4],
        summed[5],
        qk_total,
    )


def solution(mesh):
    return jax.shard_map(
        on_device,
        mesh=mesh,
        in_specs=(
            P("fsdp", "ctx", None),
            P("fsdp", "ctx", None),
            P("fsdp"),
            P("fsdp", None),
            P("fsdp", None),
            P("fsdp", None, None),
            P("fsdp", None),
            P("fsdp"),
            P("fsdp"),
            P(),
        ),
        out_specs=(
            P("fsdp", "ctx", None),
            P("fsdp", "ctx", None),
            P("fsdp", None),
            P("fsdp", None),
            P("fsdp", None, None),
            P("fsdp", None),
            P("fsdp"),
            P("fsdp"),
            P(),
        ),
        check_vma=False,
    )
```

profile of v0, /device:TPU:0, one launch (start us, length us, event | category | flops | bytes accessed | tf_op | source)
XLA Modules:
  0.0 2385.9 jit_solution(13541562072520986390)
XLA Ops:
  8.6 22.5 all-gather
  34.1 77.8 %all-gather.8.cloned.1.call-done = bf16[2048,1536]{1,0:T(8,128)(2,1)} async-done(((bf16[256,1536]{1,0:T(8,128)(2,1)}), bf16[2048,1536]{1,0:T(8,128)(2,1)}) %all-gather.8.cloned.1.call-update) | async-done | bytes 6291472 | tf_op jit(solution)/shard_map/all_gather | solution.py:95
  128.4 17.9 all-gather.1
  157.6 25.6 %while.47 = (s32[]{:T(128)}, f32[4,4,256]{2,1,0:T(4,128)S(1)}, f32[4,4,256]{2,1,0:T(4,128)S(1)}, s32[2]{0:T(128)S(1)}, s32[]{:T(128)}, /*index=5*/bf16[2,512,2,4...) while((s32[]{:T(128)}, f32[4,4,256]{2,1,0:T(4,128)S(1)}, ...), condition=%wide.region_6.7_spmd.clone, body=%wide.region_3.6_spmd.clone.sunk | while | flops 283399936 | bytes 19225752 | solution.py:140
  183.2 13.6 while.48
  198.1 12.3 all-gather.12.cloned.1.call-done
  215.3 633.1 %all-gather.14.cloned.1.call-done = bf16[2048,2,4096]{2,0,1:T(8,128)(2,1)} async-done(((bf16[256,2,4096]{2,0,1:T(8,128)(2,1)}), bf16[2048,2,4096]{2,0,1:T(8,128)(2,1)}) %all-gather.14.cloned.1.call-update) | async-done | bytes 33554448 | tf_op jit(solution)/shard_map/all_gather | solution.py:170
  848.4 20.3 fusion.110
  868.8 209.3 %all-gather.16.cloned.1.call-done = bf16[4096,2048]{1,0:T(8,128)(2,1)} async-done(((bf16[512,2048]{1,0:T(8,128)(2,1)}), bf16[4096,2048]{1,0:T(8,128)(2,1)}) %all-gather.16.cloned.1.call-update) | async-done | bytes 16777232 | tf_op jit(solution)/shard_map/all_gather | solution.py:178
  1078.0 13.2 multiply_bitcast_fusion
  1091.3 18.9 multiply_reduce_fusion
  1119.4 29.0 %while.46 = (s32[]{:T(128)}, bf16[2,512,512]{2,1,0:T(8,128)(2,1)}, s32[2]{0:T(128)S(1)}, s32[]{:T(128)}, bf16[2,512,2,4,64]{1,4,3,2,0:T(8,128)(2,1)S(1)}, /*inde...) while((s32[]{:T(128)}, bf16[2,512,512]{2,1,0:T(8,128)(2,1)}, ...), condition=%wide.region_13.14_spmd.clone, body=%wide.region_12.13_spmd.clone.sunk | while | flops 1096288000 | bytes 68607184 | solution.py:264
  1154.5 30.2 %while.49 = (s32[]{:T(128)}, f32[256,4,4,64]{0,3,2,1:T(8,128)}, bf16[2,512,2,4,64]{1,4,3,2,0:T(8,128)(2,1)S(1)}, s32[2]{0:T(128)S(1)}, s32[]{:T(128)}, /*index=5...) while((s32[]{:T(128)}, f32[256,4,4,64]{0,3,2,1:T(8,128)}, ...), condition=%wide.region_17.18_spmd.clone, body=%wide.region_16.17_spmd.clone.sunk | while | flops 818677504 | bytes 22060200 | solution.py:238
  1198.7 12.5 convolution_convert_fusion.1
  1212.8 17.8 convolution_convert_fusion
  1230.7 33.2 %reduce-scatter.10.cloned.1.call-done = bf16[128,2048]{1,0:T(8,128)(2,1)} async-done(((bf16[1024,2048]{1,0:T(8,128)(2,1)}), bf16[128,2048]{1,0:T(8,128)(2,1)}) %reduce-scatter.10.cloned.1.call-update) | async-done | bytes 524304 | tf_op jit(solution)/shard_map/reduce_scatter | solution.py:284
  1263.9 121.3 %reduce-scatter.8.cloned.1.call-done = bf16[256,1536]{1,0:T(8,128)(2,1)} async-done(((bf16[2048,1536]{1,0:T(8,128)(2,1)}), bf16[256,1536]{1,0:T(8,128)(2,1)}) %reduce-scatter.8.cloned.1.call-update) | async-done | bytes 786448 | tf_op jit(solution)/shard_map/reduce_scatter | solution.py:281
  1385.2 285.7 %reduce-scatter.14.cloned.1.call-done = bf16[512,2048]{1,0:T(8,128)(2,1)} async-done(((bf16[4096,2048]{1,0:T(8,128)(2,1)}), bf16[512,2048]{1,0:T(8,128)(2,1)}) %reduce-scatter.14.cloned.1.call-update) | async-done | bytes 2097168 | tf_op jit(solution)/shard_map/reduce_scatter | solution.py:184
  1671.0 546.2 %reduce-scatter.12.cloned.1.call-done = bf16[256,2,4096]{2,0,1:T(8,128)(2,1)} async-done(((bf16[2048,2,4096]{2,0,1:T(8,128)(2,1)}), bf16[256,2,4096]{2,0,1:T(8,128)(2,1)}) %reduce-scatter.12.cloned.1.call-update) | async-done | bytes 4194320 | tf_op jit(solution)/shard_map/reduce_scatter | solution.py:193
  2218.4 15.3 fusion.83
  2240.6 19.1 all-reduce.13
  2268.2 38.0 %psum.55 = f32[2,64]{1,0:T(2,128)} all-reduce(f32[2,64]{1,0:T(2,128)S(1)} %pad_add_fusion.2), channel_id=1, replica_groups=mesh['fsdp'=8,'ctx'=4] {'fsdp','ctx'}, use_global_device_ids=true, to_apply=%region_36.37 | all-reduce | flops 128 | bytes 1024 | tf_op jit(solution)/shard_map/psum | solution.py:302
  2310.1 51.8 %all-reduce.18.cloned.1.call-done = (bf16[256,2,4096]{2,0,1:T(8,128)(2,1)}, bf16[256,1536]{1,0:T(8,128)(2,1)}, bf16[128,2048]{1,0:T(8,128)(2,1)}, bf16[512,2048]{1,0:T(8,128)(2,1)}) async-done(((bf16[256,2,4096]{2,0,1:T(8,128)(2,1)}, bf16[256,1536]{1,0:T(8,128)(2,1)}, bf16[128,2048]{1,0:T(8,128)(2,1)}, bf16[512,2048]{1,0:T(8,128)(2,1)}), (bf16[256,2,4096]{2,0,1:T(8,128)(2,1)}, bf16[256,1536]{1,0:T(8,128)(2,1)}, ...) | async-done | bytes 7602192 | tf_op jit(solution)/shard_map/psum | solution.py:297
  2366.5 10.1 copy.74
  (281 shorter events, 192.2 us)
Async XLA Ops:
  7.2 104.8 %all-gather.8.cloned.1.call-start = ((), (), s32[]{:S(2)}) async-start(), calls=%async_computation.5 | async-start | bytes 7077888 | tf_op jit(solution)/shard_map/all_gather | solution.py:95
  7.9 142.1 %all-gather.10.cloned.1.call-start = ((), (), s32[]{:S(2)}) async-start(), calls=%async_computation.6 | async-start | bytes 1310720 | tf_op jit(solution)/shard_map/all_gather | solution.py:114
  31.1 85.8 %copy-start.27 = (f32[8,1,256]{2,1,0:T(1,128)}, f32[8,1,256]{2,1,0:T(1,128)S(1)}, u32[]{:S(2)}) copy-start(f32[8,1,256]{2,1,0:T(1,128)S(1)} %convert_element_type.220) | copy-start | bytes 24580
  33.9 83.1 %copy-start.36 = (f32[256]{0:T(256)}, f32[256]{0:T(256)S(1)}, u32[]{:S(2)}) copy-start(f32[256]{0:T(256)S(1)} %fusion.115) | copy-start | bytes 3076
  33.9 84.4 %copy-start.41 = (f32[64]{0:T(128)}, f32[64]{0:T(128)S(1)}, u32[]{:S(2)}) copy-start(f32[64]{0:T(128)S(1)} %get-tuple-element.562) | copy-start | bytes 772
  33.9 114.9 %copy-start.43 = (f32[64]{0:T(128)}, f32[64]{0:T(128)S(1)}, u32[]{:S(2)}) copy-start(f32[64]{0:T(128)S(1)} %get-tuple-element.561) | copy-start | bytes 772
  34.1 115.7 %copy-start.21 = (f32[256,32]{0,1:T(8,128)}, f32[256,32]{0,1:T(8,128)S(1)}, u32[]{:S(2)}) copy-start(f32[256,32]{0,1:T(8,128)S(1)} %get-tuple-element.559) | copy-start | bytes 98308
  34.1 115.7 %copy-start.23 = (f32[256,32]{0,1:T(8,128)}, f32[256,32]{0,1:T(8,128)S(1)}, u32[]{:S(2)}) copy-start(f32[256,32]{0,1:T(8,128)S(1)} %get-tuple-element.560) | copy-start | bytes 98308
  119.8 90.6 %all-gather.12.cloned.1.call-start = ((), (), s32[]{:S(2)}) async-start(), calls=%async_computation.7 | async-start | bytes 4718592 | tf_op jit(solution)/shard_map/all_gather | solution.py:96
  120.6 727.9 %all-gather.14.cloned.1.call-start = ((), (), s32[]{:S(2)}) async-start(), calls=%async_computation.8 | async-start | bytes 37748736 | tf_op jit(solution)/shard_map/all_gather | solution.py:170
  127.7 950.3 %all-gather.16.cloned.1.call-start = ((), (), s32[]{:S(2)}) async-start(), calls=%async_computation.9 | async-start | bytes 18874368 | tf_op jit(solution)/shard_map/all_gather | solution.py:178
  128.3 1062.0 %reduce-scatter.6.cloned.1.call-start = ((), (), s32[]{:S(2)}) async-start(), calls=%async_computation.10 | async-start | bytes 1310720 | tf_op jit(solution)/shard_map/reduce_scatter | solution.py:263
  147.0 963.2 %copy-start.45 = (f32[256]{0:T(256)}, f32[256]{0:T(256)S(1)}, u32[]{:S(2)}) copy-start(f32[256]{0:T(256)S(1)} %compare_convert_fusion) | copy-start | bytes 3076
  215.3 894.9 %copy-start.31 = (f32[256]{0:T(256)}, f32[256]{0:T(256)S(1)}, u32[]{:S(2)}) copy-start(f32[256]{0:T(256)S(1)} %fusion.116) | copy-start | bytes 3076
  848.4 229.6 %copy-start.19 = (bf16[1,256,2048]{2,1,0:T(8,128)(2,1)S(1)}, bf16[1,256,2048]{2,1,0:T(8,128)(2,1)}, u32[]{:S(2)}) copy-start(bf16[1,256,2048]{2,1,0:T(8,128)(2,1)} %param.19) | copy-start | bytes 3145732
  1148.5 115.4 %reduce-scatter.10.cloned.1.call-start = ((), (), s32[]{:S(2)}) async-start(), calls=%async_computation.12 | async-start | bytes 4718592 | tf_op jit(solution)/shard_map/reduce_scatter | solution.py:284
  1153.4 231.8 %reduce-scatter.8.cloned.1.call-start = ((), (), s32[]{:S(2)}) async-start(), calls=%async_computation.11 | async-start | bytes 7077888 | tf_op jit(solution)/shard_map/reduce_scatter | solution.py:281
  1197.4 473.5 %reduce-scatter.14.cloned.1.call-start = ((), (), s32[]{:S(2)}) async-start(), calls=%async_computation.14 | async-start | bytes 18874368 | tf_op jit(solution)/shard_map/reduce_scatter | solution.py:184
  1211.2 1005.9 %reduce-scatter.12.cloned.1.call-start = ((), (), s32[]{:S(2)}) async-start(), calls=%async_computation.13 | async-start | bytes 37748736 | tf_op jit(solution)/shard_map/reduce_scatter | solution.py:193
  1230.7 986.5 %copy-start.49 = (u32[32]{0:T(128)S(1)}, u32[32]{0:T(128)}, u32[]{:S(2)}) copy-start(u32[32]{0:T(128)} %constant.125) | copy-start | bytes 388
  1230.7 987.7 %copy-start.47 = (f32[256]{0:T(256)S(1)}, f32[256]{0:T(256)}, u32[]{:S(2)}) copy-start(f32[256]{0:T(256)} %copy-done.45) | copy-start | bytes 3076
  1230.7 1131.2 %all-reduce.18.cloned.1.call-start = ((), (), s32[]{:S(2)}) async-start(), calls=%async_computation.15 | async-start | bytes 15204352 | tf_op jit(solution)/shard_map/psum | solution.py:297
  2233.8 72.4 %copy-start.40 = (f32[256]{0:T(256)S(1)}, f32[256]{0:T(256)}, u32[]{:S(2)}) copy-start(f32[256]{0:T(256)} %copy-done.39) | copy-start | bytes 3076
  2233.8 73.1 %copy-start.8 = (f32[256,2048]{1,0:T(8,128)S(1)}, f32[256,2048]{1,0:T(8,128)}, u32[]{:S(2)}) copy-start(f32[256,2048]{1,0:T(8,128)} %copy-done.7) | copy-start | bytes 6291460
  (39 other events, 248.2 us)
Sparse Core Ops, SparseCore 0:
  10.2 101.7 all-gather.7
  119.9 14.9 all-gather.9
  137.0 73.3 all-gather.11
  212.4 635.9 all-gather.13
  850.4 227.5 all-gather.15
  1148.6 23.0 reduce-scatter.5
  1175.8 88.0 reduce-scatter.9
  1267.5 117.7 reduce-scatter.7
  1389.0 281.8 reduce-scatter.13
  1675.0 542.0 reduce-scatter.11
  2219.8 142.0 all-reduce.17
where the time goes:
time: 2390 us
  waiting for transfers between devices  1970 us (82%)
  matrix products  189 us (8%)
  blocking collectives  104 us (4%)
  other arithmetic  55.1 us (2%)
  local copies, waits for them, and re-layouts  47.4 us (2%)
    all_gather x1, waiting for transfers between devices, on_device(): lax.all_gather(gate_up, 'fsdp', axis=0, tiled=True)  633 us
    reduce_scatter x1, waiting for transfers between devices, on_device(): lax.psum_scatter(jnp.einsum('td,tgf->dgf', columns, d_proj_low, preferred...  546 us
    reduce_scatter x1, waiting for transfers between devices, on_device(): lax.psum_scatter(contract_rows(hidden, d_out_low).astype(jnp.bfloat16), '...  286 us
    all_gather x1, waiting for transfers between devices, on_device(): lax.all_gather(down_weight, 'fsdp', axis=0, tiled=True)  209 us
    reduce_scatter x1, waiting for transfers between devices, on_device(): lax.psum_scatter(qkv_term.astype(jnp.bfloat16), 'fsdp', scatter_dimension...  121 us
    all_gather x1, waiting for transfers between devices, on_device(): lax.all_gather(qkv_weight, 'fsdp', axis=0, tiled=True)  77.8 us
    psum x1, waiting for transfers between devices, on_device(): lax.psum(gate_up_shard, 'ctx').astype(jnp.float32)  51.8 us
  transfers between devices with their start and end apart: 11, of which 9 were waited for; matrix products, arithmetic and copies ran while one was open for 8% of the time, Pallas kernels for 0%

commit v1 on v0

--- a/solution.py
+++ b/solution.py
@@ -8,6 +8,19 @@
 KV_HEADS = 4
 HEAD_DIM = 64
 EPSILON = 1e-06
+
+
+def pass_the_plate(point):
+    passed = jax.lax.psum(1, "fsdp")
+    arr_now = jax.lax.axis_index("fsdp")
+    row_out, y_new, f_next = (passed, arr_now, point.shape[0])
+    view_out, part_next = (point, 1)
+    while part_next < row_out:
+        latest = tuple(((ix, (ix - part_next) % row_out) for ix in range(row_out)))
+        prior = jax.lax.ppermute(view_out, "fsdp", latest)
+        view_out = jnp.concatenate([view_out, prior], 0)
+        part_next = 2 * part_next
+    return jnp.roll(view_out, y_new * f_next, 0)
 
 
 def root_norm(values, norm_gain):
@@ -165,10 +178,7 @@
     normed_mid = root_norm(middle, ffn_norm).astype(jnp.bfloat16)
     columns = normed_mid
     projected = jnp.einsum(
-        "td,dgf->tgf",
-        columns,
-        lax.all_gather(gate_up, "fsdp", axis=0, tiled=True),
-        preferred_element_type=jnp.float32,
+        "td,dgf->tgf", columns, pass_the_plate(gate_up), preferred_element_type=jnp.float32
     )
     act_value, act_pull = jax.vjp(activate, projected)
     hidden = act_value.astype(jnp.bfloat16)

time: 2390 us -> 3150 us (1.32)
  blocking collectives: 104 us -> 501 us
  waiting for transfers between devices: 1970 us -> 2240 us
  local copies, waits for them, and re-layouts: 47.4 us -> 104 us
    ppermute x0 -> x3, waiting for transfers between devices: none -> 1000 us  [pass_the_plate(): prior = jax.lax.ppermute(view_out, 'fsdp', latest)]
    all_gather x1, waiting for transfers between devices: 633 us -> 71.4 us  [on_device(): lax.all_gather(gate_up, 'fsdp', axis=0, tiled=True)]
    all_gather x1, blocking collectives: 17.9 us -> 415 us  [on_device(): lax.all_gather(ffn_gain, 'fsdp', axis=0, tiled=True)]
    all_gather x1, waiting for transfers between devices: 209 us -> 0.01 us  [on_device(): lax.all_gather(down_weight, 'fsdp', axis=0, tiled=True)]
    reduce_scatter x1, waiting for transfers between devices: 33.2 us -> 91.1 us  [on_device(): lax.psum_scatter(out_term.astype(jnp.bfloat16), 'fsdp', scatter_dimension...]
    unnamed x104 -> x118, local copies, waits for them, and re-layouts: 29.6 us -> 74.5 us
  transfers between devices with their start and end apart: 11 -> 14, of which waited for: 9 -> 11; matrix products, arithmetic and copies ran while one was open for 8% -> 9% of each run, Pallas kernels for 0% -> 0%
where the time goes in v1:
time: 3150 us; the launch traced here: 3140 us
  waiting for transfers between devices  2240 us (71%)
  blocking collectives  501 us (16%)
  matrix products  199 us (6%)
  local copies, waits for them, and re-layouts  104 us (3%)
  other arithmetic  72.4 us (2%)
    ppermute x3, waiting for transfers between devices, pass_the_plate(): prior = jax.lax.ppermute(view_out, 'fsdp', latest)  1000 us
    reduce_scatter x1, waiting for transfers between devices, on_device(): lax.psum_scatter(jnp.einsum('td,tgf->dgf', columns, d_proj_low, preferred...  546 us
    all_gather x1, blocking collectives, on_device(): lax.all_gather(ffn_gain, 'fsdp', axis=0, tiled=True)  415 us
    reduce_scatter x1, waiting for transfers between devices, on_device(): lax.psum_scatter(contract_rows(hidden, d_out_low).astype(jnp.bfloat16), '...  260 us
    reduce_scatter x1, waiting for transfers between devices, on_device(): lax.psum_scatter(qkv_term.astype(jnp.bfloat16), 'fsdp', scatter_dimension...  122 us
    reduce_scatter x1, waiting for transfers between devices, on_device(): lax.psum_scatter(out_term.astype(jnp.bfloat16), 'fsdp', scatter_dimension...  91.1 us
    all_gather x1, waiting for transfers between devices, on_device(): lax.all_gather(qkv_weight, 'fsdp', axis=0, tiled=True)  77.8 us
    unnamed x118, local copies, waits for them, and re-layouts  74.5 us
  transfers between devices with their start and end apart: 14, of which 11 were waited for; matrix products, arithmetic and copies ran while one was open for 9% of the time, Pallas kernels for 0%

profile of v1, /device:TPU:0, one launch (start us, length us, event | category | flops | bytes accessed | tf_op | source)
XLA Modules:
  0.0 3138.1 jit_solution(1857989905166265707)
XLA Ops:
  8.6 22.5 all-gather
  34.2 77.8 %all-gather.8.cloned.1.call-done = bf16[2048,1536]{1,0:T(8,128)(2,1)} async-done(((bf16[256,1536]{1,0:T(8,128)(2,1)}), bf16[2048,1536]{1,0:T(8,128)(2,1)}) %all-gather.8.cloned.1.call-update) | async-done | bytes 6291472 | tf_op jit(solution)/shard_map/all_gather | solution.py:108
  131.3 107.2 %collective-permute-done = bf16[256,2,4096]{2,0,1:T(8,128)(2,1)} collective-permute-done((bf16[256,2,4096]{2,0,1:T(8,128)(2,1)}, bf16[256,2,4096]{2,0,1:T(8,128)(2,1)}, u32[]{:S(2)}, u32[]{:S(2)}) %collective-permute-start) | collective-permute-done | bytes 4194336 | tf_op jit(solution)/shard_map/ppermute | solution.py:20
  247.3 212.4 %collective-permute-done.1 = bf16[512,2,4096]{2,0,1:T(8,128)(2,1)S(1)} collective-permute-done((bf16[512,2,4096]{2,0,1:T(8,128)(2,1)}, bf16[512,2,4096]{2,0,1:T(8,128)(2,1)S(1)}, u32[]{:S(2)}, u32[]{:S(2)}) %collective-permute-start.1) | collective-permute-done | bytes 8388640 | tf_op jit(solution)/shard_map/ppermute | solution.py:20
  473.7 414.8 %all-gather.1 = bf16[8,1,256]{2,1,0:T(2,128)(2,1)S(1)} all-gather(bf16[1,1,256]{2,1,0:T(2,128)(2,1)S(1)} %reshape.283), channel_id=1, replica_groups=mesh['fsdp'=8,'ctx'=4] {'fsdp'}, dimensions={0}, use_global_device_ids=true | all-gather | bytes 4608 | tf_op jit(solution)/shard_map/all_gather | solution.py:111
  911.3 25.3 while.47
  956.7 680.8 %collective-permute-done.2 = bf16[1024,2,4096]{2,0,1:T(8,128)(2,1)} collective-permute-done((bf16[1024,2,4096]{2,0,1:T(8,128)(2,1)}, bf16[1024,2,4096]{2,0,1:T(8,128)(2,1)}, u32[]{:S(2)}, u32[]{:S(2)}) %collective-permute-start.2) | collective-permute-done | bytes 16777248 | tf_op jit(solution)/shard_map/ppermute | solution.py:20
  1637.5 14.6 constant_dynamic-update-slice_fusion.5
  1669.5 14.0 constant_dynamic-update-slice_fusion.1
  1683.5 18.2 fusion.72
  1715.0 71.4 %all-gather.16.cloned.1.call-done = bf16[2048,2,4096]{2,0,1:T(8,128)(2,1)} async-done(((bf16[256,2,4096]{2,0,1:T(8,128)(2,1)}), bf16[2048,2,4096]{2,0,1:T(8,128)(2,1)}) %all-gather.16.cloned.1.call-update) | async-done | bytes 33554448 | tf_op jit(solution)/shard_map/all_gather | solution.py:214
  1786.4 19.0 multiply_reduce_fusion
  1812.7 41.0 %while.46 = (s32[]{:T(128)}, bf16[2,512,512]{2,1,0:T(8,128)(2,1)}, s32[2]{0:T(128)S(1)}, s32[]{:T(128)}, bf16[2,512,2,4,64]{1,4,3,2,0:T(8,128)(2,1)S(1)}, /*inde...) while((s32[]{:T(128)}, bf16[2,512,512]{2,1,0:T(8,128)(2,1)}, ...), condition=%wide.region_13.14_spmd.clone, body=%wide.region_12.13_spmd.clone.sunk | while | flops 1096288000 | bytes 32956044 | solution.py:274
  1871.1 30.5 while.49
  1907.2 18.3 reduce-scatter.6.cloned.1.call-done
  1933.9 18.8 convolution_convert_fusion
  1952.8 259.7 %reduce-scatter.14.cloned.1.call-done = bf16[512,2048]{1,0:T(8,128)(2,1)} async-done(((bf16[4096,2048]{1,0:T(8,128)(2,1)}), bf16[512,2048]{1,0:T(8,128)(2,1)}) %reduce-scatter.14.cloned.1.call-update) | async-done | bytes 2097168 | tf_op jit(solution)/shard_map/reduce_scatter | solution.py:194
  2212.6 91.1 %reduce-scatter.10.cloned.1.call-done = bf16[128,2048]{1,0:T(8,128)(2,1)} async-done(((bf16[1024,2048]{1,0:T(8,128)(2,1)}), bf16[128,2048]{1,0:T(8,128)(2,1)}) %reduce-scatter.10.cloned.1.call-update) | async-done | bytes 524304 | tf_op jit(solution)/shard_map/reduce_scatter | solution.py:294
  2303.7 121.8 %reduce-scatter.8.cloned.1.call-done = bf16[256,1536]{1,0:T(8,128)(2,1)} async-done(((bf16[2048,1536]{1,0:T(8,128)(2,1)}), bf16[256,1536]{1,0:T(8,128)(2,1)}) %reduce-scatter.8.cloned.1.call-update) | async-done | bytes 786448 | tf_op jit(solution)/shard_map/reduce_scatter | solution.py:291
  2425.5 546.2 %reduce-scatter.12.cloned.1.call-done = bf16[256,2,4096]{2,0,1:T(8,128)(2,1)} async-done(((bf16[2048,2,4096]{2,0,1:T(8,128)(2,1)}), bf16[256,2,4096]{2,0,1:T(8,128)(2,1)}) %reduce-scatter.12.cloned.1.call-update) | async-done | bytes 4194320 | tf_op jit(solution)/shard_map/reduce_scatter | solution.py:203
  2973.0 15.3 fusion.85
  2995.2 19.0 all-reduce.13
  3022.7 37.9 %psum.55 = f32[2,64]{1,0:T(2,128)} all-reduce(f32[2,64]{1,0:T(2,128)S(1)} %pad_add_fusion.2), channel_id=1, replica_groups=mesh['fsdp'=8,'ctx'=4] {'fsdp','ctx'}, use_global_device_ids=true, to_apply=%region_36.37 | all-reduce | flops 128 | bytes 1024 | tf_op jit(solution)/shard_map/psum | solution.py:312
  3064.5 51.8 %all-reduce.18.cloned.1.call-done = (bf16[256,2,4096]{2,0,1:T(8,128)(2,1)}, bf16[256,1536]{1,0:T(8,128)(2,1)}, bf16[128,2048]{1,0:T(8,128)(2,1)}, bf16[512,2048]{1,0:T(8,128)(2,1)}) async-done(((bf16[256,2,4096]{2,0,1:T(8,128)(2,1)}, bf16[256,1536]{1,0:T(8,128)(2,1)}, bf16[128,2048]{1,0:T(8,128)(2,1)}, bf16[512,2048]{1,0:T(8,128)(2,1)}), (bf16[256,2,4096]{2,0,1:T(8,128)(2,1)}, bf16[256,1536]{1,0:T(8,128)(2,1)}, ...) | async-done | bytes 7602192 | tf_op jit(solution)/shard_map/psum | solution.py:307
  (296 shorter events, 302.3 us)
Async XLA Ops:
  7.2 104.8 %all-gather.8.cloned.1.call-start = ((), (), s32[]{:S(2)}) async-start(), calls=%async_computation.5 | async-start | bytes 7077888 | tf_op jit(solution)/shard_map/all_gather | solution.py:108
  7.9 895.8 %all-gather.10.cloned.1.call-start = ((), (), s32[]{:S(2)}) async-start(), calls=%async_computation.6 | async-start | bytes 1310720 | tf_op jit(solution)/shard_map/all_gather | solution.py:127
  31.1 85.8 %copy-start.30 = (f32[8,1,256]{2,1,0:T(1,128)}, f32[8,1,256]{2,1,0:T(1,128)S(1)}, u32[]{:S(2)}) copy-start(f32[8,1,256]{2,1,0:T(1,128)S(1)} %convert_element_type.220) | copy-start | bytes 24580
  34.0 860.8 %copy-start.46 = (f32[64]{0:T(128)}, f32[64]{0:T(128)S(1)}, u32[]{:S(2)}) copy-start(f32[64]{0:T(128)S(1)} %get-tuple-element.563) | copy-start | bytes 772
  34.2 861.5 %copy-start.22 = (f32[256,32]{0,1:T(8,128)}, f32[256,32]{0,1:T(8,128)S(1)}, u32[]{:S(2)}) copy-start(f32[256,32]{0,1:T(8,128)S(1)} %get-tuple-element.561) | copy-start | bytes 98308
  34.2 861.5 %copy-start.24 = (f32[256,32]{0,1:T(8,128)}, f32[256,32]{0,1:T(8,128)S(1)}, u32[]{:S(2)}) copy-start(f32[256,32]{0,1:T(8,128)S(1)} %get-tuple-element.562) | copy-start | bytes 98308
  119.8 831.8 %all-gather.12.cloned.1.call-start = ((), (), s32[]{:S(2)}) async-start(), calls=%async_computation.7 | async-start | bytes 4718592 | tf_op jit(solution)/shard_map/all_gather | solution.py:109
  120.6 1581.2 %all-gather.14.cloned.1.call-start = ((), (), s32[]{:S(2)}) async-start(), calls=%async_computation.8 | async-start | bytes 18874368 | tf_op jit(solution)/shard_map/all_gather | solution.py:188
  121.1 1665.3 %all-gather.16.cloned.1.call-start = ((), (), s32[]{:S(2)}) async-start(), calls=%async_computation.9 | async-start | bytes 37748736 | tf_op jit(solution)/shard_map/all_gather | solution.py:214
  129.7 1795.9 %reduce-scatter.6.cloned.1.call-start = ((), (), s32[]{:S(2)}) async-start(), calls=%async_computation.10 | async-start | bytes 1310720 | tf_op jit(solution)/shard_map/reduce_scatter | solution.py:273
  129.8 108.7 %collective-permute-start = (bf16[256,2,4096]{2,0,1:T(8,128)(2,1)}, bf16[256,2,4096]{2,0,1:T(8,128)(2,1)}, u32[]{:S(2)}, u32[]{:S(2)}) collective-permute-start(bf16[256,2,4096]{2,0,1:T(8,128)(2,1)} %get-tuple-element.549), channel_id=1, source_target_pairs={{0,28},{4,0},{8,4},{12,8},{16,12},{20,16},{24,20},{28,24},{1,29},{... | collective-permute-start | bytes 12582920 | tf_op jit(solution)/shard_map/ppermute | solution.py:20
  246.4 227.2 %copy-start.50 = (bf16[256]{0:T(256)(128)(2,1)S(1)}, bf16[256]{0:T(256)(128)(2,1)}, u32[]{:S(2)}) copy-start(bf16[256]{0:T(256)(128)(2,1)} %param.26) | copy-start | bytes 1540
  246.4 213.3 %collective-permute-start.1 = (bf16[512,2,4096]{2,0,1:T(8,128)(2,1)}, bf16[512,2,4096]{2,0,1:T(8,128)(2,1)S(1)}, u32[]{:S(2)}, u32[]{:S(2)}) collective-permute-start(bf16[512,2,4096]{2,0,1:T(8,128)(2,1)} %pad_maximum_fusion.1), channel_id=1, source_target_pairs={{0,24},{4,28},{8,0},{12,4},{16,8},{20,12},{24,16},{28,20},{1,25},{... | collective-permute-start | bytes 25165832 | tf_op jit(solution)/shard_map/ppermute | solution.py:20
  472.3 1165.2 %collective-permute-start.2 = (bf16[1024,2,4096]{2,0,1:T(8,128)(2,1)}, bf16[1024,2,4096]{2,0,1:T(8,128)(2,1)}, u32[]{:S(2)}, u32[]{:S(2)}) collective-permute-start(bf16[1024,2,4096]{2,0,1:T(8,128)(2,1)} %pad_maximum_fusion), channel_id=1, source_target_pairs={{0,16},{4,20},{8,24},{12,28},{16,0},{20,4},{24,8},{28,12},{1,17},{... | collective-permute-start | bytes 50331656 | tf_op jit(solution)/shard_map/ppermute | solution.py:20
  889.2 964.6 %copy-start.48 = (f32[256]{0:T(256)}, f32[256]{0:T(256)S(1)}, u32[]{:S(2)}) copy-start(f32[256]{0:T(256)S(1)} %compare_convert_fusion) | copy-start | bytes 3076
  956.7 848.7 %copy-start.38 = (f32[256]{0:T(256)}, f32[256]{0:T(256)S(1)}, u32[]{:S(2)}) copy-start(f32[256]{0:T(256)S(1)} %fusion.117) | copy-start | bytes 3076
  956.7 695.4 %copy-start.9 = (bf16[256,2,4096]{2,1,0:T(2,128)(2,1)S(1)}, bf16[256,2,4096]{2,1,0:T(2,128)(2,1)}, u32[]{:S(2)}) copy-start(bf16[256,2,4096]{2,1,0:T(2,128)(2,1)} %param.23) | copy-start | bytes 12582916
  1853.8 358.8 %reduce-scatter.14.cloned.1.call-start = ((), (), s32[]{:S(2)}) async-start(), calls=%async_computation.14 | async-start | bytes 18874368 | tf_op jit(solution)/shard_map/reduce_scatter | solution.py:194
  1865.1 438.6 %reduce-scatter.10.cloned.1.call-start = ((), (), s32[]{:S(2)}) async-start(), calls=%async_computation.12 | async-start | bytes 4718592 | tf_op jit(solution)/shard_map/reduce_scatter | solution.py:294
  1871.0 554.5 %reduce-scatter.8.cloned.1.call-start = ((), (), s32[]{:S(2)}) async-start(), calls=%async_computation.11 | async-start | bytes 7077888 | tf_op jit(solution)/shard_map/reduce_scatter | solution.py:291
  1932.4 1039.3 %reduce-scatter.12.cloned.1.call-start = ((), (), s32[]{:S(2)}) async-start(), calls=%async_computation.13 | async-start | bytes 37748736 | tf_op jit(solution)/shard_map/reduce_scatter | solution.py:203
  1952.8 1019.0 %copy-start.51 = (u32[32]{0:T(128)S(1)}, u32[32]{0:T(128)}, u32[]{:S(2)}) copy-start(u32[32]{0:T(128)} %constant.151) | copy-start | bytes 388
  1952.8 1020.2 %copy-start.49 = (f32[256]{0:T(256)S(1)}, f32[256]{0:T(256)}, u32[]{:S(2)}) copy-start(f32[256]{0:T(256)} %copy-done.48) | copy-start | bytes 3076
  1952.8 1163.5 %all-reduce.18.cloned.1.call-start = ((), (), s32[]{:S(2)}) async-start(), calls=%async_computation.15 | async-start | bytes 15204352 | tf_op jit(solution)/shard_map/psum | solution.py:307
  (42 other events, 716.6 us)
Sparse Core Ops, SparseCore 0:
  10.2 101.7 all-gather.7
  119.9 14.8 all-gather.9
  137.0 171.7 all-gather.11
  310.8 836.8 all-gather.13
  1149.7 636.6 all-gather.15
  1853.9 71.6 reduce-scatter.5
  1929.8 282.7 reduce-scatter.13
  2216.8 86.8 reduce-scatter.9
  2307.7 117.7 reduce-scatter.7
  2429.6 542.0 reduce-scatter.11
  2974.4 141.8 all-reduce.17
